TPU v7x, 128 devices: a whole 4x4x4 slice. The times are simulated.
128 devices in a mesh: sx: 8 (over z, core), sy: 8 (over x_lo, y), rep: 2 (over x_hi).
Axes of the slice: x: 4 (x_hi: 2, x_lo: 2; x = x_hi * 2 + x_lo), y: 4, z: 4, core: 2. Of those that a mesh axis runs over, the one named last changes fastest.
Arguments:
- volume: bfloat16 [2, 32, 16, 128, 256], P('rep', None, 'sx', 'sy'), may hold values from -6 to 6
- first_kernel: bfloat16 [64, 32, 3, 3, 3], replicated, may hold values from -0.21875 to 0.21875
- first_bias: float32 [64], replicated, may hold values from -3 to 3
- second_kernel: bfloat16 [128, 64, 3, 3, 3], P('sy'), may hold values from -0.15625 to 0.15625
- second_bias: float32 [128], P('sy'), may hold values from -3 to 3
- cotangent: bfloat16 [2, 128, 8, 64, 128], P('rep', 'sy', 'sx'), may hold values from -6 to 6
Outputs:
- second_out: float32 [2, 128, 8, 64, 128], P('rep', 'sy', 'sx')
- grad_first_kernel: float32 [64, 32, 3, 3, 3], replicated
- grad_first_bias: float32 [64], replicated
- grad_second_kernel: float32 [128, 64, 3, 3, 3], P('sy')
- grad_second_bias: float32 [128], P('sy')
All inputs are finite; a program needn't handle non-finite values.
Results may differ from a plain program's by a relative error of at most 0.0045.
Values may be sent and summed in bfloat16 or wider, within the bound.
A program may use at most 128 MiB of HBM per device.

v0:
```python
import math
import jax
import jax.numpy as jnp
from jax import lax
from jax.sharding import PartitionSpec as P


def padded_2(cells, sides, width):
    for axis, dim in sides:
        count = lax.axis_size(axis)
        ends = count - 1
        head = lax.slice_in_dim(cells, 0, width, axis=dim)
        tail = lax.slice_in_dim(cells, cells.shape[dim] - width, cells.shape[dim], axis=dim)
        cells = jnp.concatenate(
            [
                lax.ppermute(tail, axis, [(i, (i + 1) % count) for i in range(ends)]),
                cells,
                lax.ppermute(head, axis, [((i + 1) % count, i) for i in range(ends)]),
            ],
            axis=dim,
        )
    return cells


def convolve(padded, kernel, z_pad):
    return lax.conv_general_dilated(
        padded[None],
        kernel,
        (1, 1, 1),
        ((0, 0), (0, 0), (z_pad, z_pad)),
        dimension_numbers=("NCDHW", "OIDHW", "NCDHW"),
        preferred_element_type=jnp.float32,
    )[0]


def weight_terms(cotan, padded):
    cells_x, cells_y, cells_z = (cotan.shape[1], cotan.shape[2], cotan.shape[3])
    terms = []
    for i in range(3):
        for j in range(3):
            for k in range(3):
                piece = padded[:, i : i + cells_x, j : j + cells_y, k : k + cells_z]
                terms.append(
                    jnp.einsum("oxyz,cxyz->oc", cotan, piece, preferred_element_type=jnp.float32)
                )
    stacked = jnp.stack(terms).reshape(3, 3, 3, cotan.shape[0], padded.shape[0])
    return stacked.transpose(3, 4, 0, 1, 2)


def pool_mean(field):
    chans, cells_x, cells_y, cells_z = field.shape
    blocks = field.astype(jnp.float32).reshape(
        chans, cells_x // 2, 2, cells_y // 2, 2, cells_z // 2, 2
    )
    return jnp.mean(blocks, axis=(2, 4, 6))


def per_device(volume, first_kernel, first_bias, second_kernel, second_bias, cotangent):
    source = volume[0]
    cotan = cotangent[0]
    half_x, half_y, half_z = (source.shape[1] // 2, source.shape[2] // 2, source.shape[3] // 2)
    count = (
        lax.axis_size("rep") * lax.axis_size("sx") * lax.axis_size("sy") * half_x * half_y * half_z
    )
    scale = 1.0 / math.sqrt(count)
    rimmed = padded_2(source, (("sx", 1), ("sy", 2)), 1)
    input_pad = jnp.pad(rimmed, ((0, 0), (0, 0), (0, 0), (1, 1)))
    pre = convolve(input_pad, first_kernel, 0) + first_bias[:, None, None, None]
    act = jnp.where(pre > 0, pre, 0.3 * pre)
    pooled = pool_mean(act).astype(jnp.bfloat16)
    pooled_x = padded_2(pooled, (("sx", 1),), 1)
    gathered = lax.all_gather(pooled_x, "sy", axis=2, tiled=True)
    pooled_pad = jnp.pad(gathered, ((0, 0), (0, 0), (1, 1), (1, 1)))
    second = convolve(pooled_pad, second_kernel, 0) + second_bias[:, None, None, None]
    second_out = second.astype(jnp.float32)
    local_w2 = weight_terms(cotan, pooled_pad)
    local_b2 = jnp.sum(cotan.astype(jnp.float32), axis=(1, 2, 3))
    cot_x = padded_2(cotan, (("sx", 1),), 1)
    cot_pad = jnp.pad(cot_x, ((0, 0), (0, 0), (1, 1), (1, 1)))
    flipped = second_kernel.transpose(1, 0, 2, 3, 4)[:, :, ::-1, ::-1, ::-1]
    partial_back = convolve(cot_pad, flipped, 0)
    back = lax.psum_scatter(partial_back, "sy", scatter_dimension=2, tiled=True)
    summed_w2, summed_b2 = lax.psum((local_w2, local_b2), ("sx", "rep"))
    spread = jnp.repeat(jnp.repeat(jnp.repeat(back, 2, axis=1), 2, axis=2), 2, axis=3)
    grad_pre = (spread * 0.125 * jnp.where(pre > 0, 1.0, 0.3)).astype(jnp.bfloat16)
    local_w1 = weight_terms(grad_pre, input_pad)
    local_b1 = jnp.sum(grad_pre.astype(jnp.float32), axis=(1, 2, 3))
    summed_w1, summed_b1 = lax.psum((local_w1, local_b1), ("sx", "sy", "rep"))
    return (
        second_out[None],
        scale * summed_w1,
        scale * summed_b1,
        scale * summed_w2,
        scale * summed_b2,
    )


def solution(mesh):
    placed = (
        P("rep", None, "sx", "sy", None),
        P(),
        P(),
        P("sy", None, None, None, None),
        P("sy"),
        P("rep", "sy", "sx", None, None),
    )
    return jax.shard_map(
        per_device,
        mesh=mesh,
        in_specs=placed,
        out_specs=(
            P("rep", "sy", "sx", None, None),
            P(),
            P(),
            P("sy", None, None, None, None),
            P("sy"),
        ),
        check_vma=False,
    )
```

profile of v0, /device:TPU:1, one launch (start us, length us, event | category | flops | bytes accessed | tf_op | source)
XLA Modules:
  0.0 535.4 jit_solution(5171773666828313169)
XLA Ops:
  7.2 1.4 copy.329
  8.7 4.9 collective-permute-start.6
  13.6 1.9 collective-permute-start.7
  15.5 4.2 collective-permute-done.6
  19.7 4.4 collective-permute-done.7
  24.1 1.5 fusion.45
  25.9 6.1 %copy.331 = bf16[16,3,66,1,8,17]{0,4,5,2,1,3:T(8,128)(2,1)} copy(bf16[16,3,66,1,8,17]{2,0,5,4,1,3:T(8,128)(2,1)S(1)} %bitcast.640) | data formatting | bytes 1723392 | tf_op jit(solution)/shard_map/conv_general_dilated | solution.py:26
  33.4 9.5 %broadcast_select_fusion = f32[1,64,8,17,64]{4,2,3,1,0:T(8,128)S(1)} fusion(pred[8,17]{0,1:T(8,128)(4,1)S(1)} %copy-done.20, bf16[16,64,3,3,3]{1,0,4,3,2:T(8,128)(2,1)S(1)} %copy-done.17, bf16[16,3,66,1,7,2]{0,4,5,2,1,3:T(8,128)(2,1)S(1)} %slice.266, bf16[16,3,66,1,8,17]{0,4,5,2,1,3:T(8,128)(2,1)} %copy.331), kind=kOutput, calls=%fused_computation.70 | convolution fusion | flops 484742656 | bytes 3234056 | tf_op jit(solution)/shard_map/conv_general_dilated | solution.py:26
  43.7 2.6 slice_bitcast_fusion.1
  47.7 1.9 collective-permute-start
  49.6 2.4 collective-permute-start.1
  52.9 4.7 collective-permute-done.1
  57.6 3.2 collective-permute-start.2
  62.1 1.4 collective-permute-done.2
  63.5 4.2 collective-permute-done.3
  67.8 1.6 fusion.276
  69.6 5.4 %reshape.246 = bf16[32,4,18,1,8,33]{5,4,0,2,1,3:T(8,128)(2,1)} reshape(bf16[32,4,18,1,264]{4,0,2,1,3:T(8,128)(2,1)S(1)} %pad.15) | data formatting | bytes 2433024 | tf_op jit(solution)/shard_map/conv_general_dilated | solution.py:26
  75.0 9.3 %copy.321 = bf16[32,4,18,1,8,33]{0,4,5,2,1,3:T(8,128)(2,1)} copy(bf16[32,4,18,1,8,33]{5,4,0,2,1,3:T(8,128)(2,1)} %reshape.246) | data formatting | bytes 2433024 | tf_op jit(solution)/shard_map/conv_general_dilated | solution.py:26
  85.4 12.4 %compare_select_fusion = (f32[2,16,8,33,64]{4,2,3,1,0:T(8,128)}, f32[2,16,8,33,64]{4,2,3,1,0:T(8,128)S(1)}, f32[2,16,8,33,64]{4,2,3,1,0:T(8,128)}) fusion(f32[64]{0:T(128)S(1)} %copy-done.15, bf16[64,32,3,3,3]{0,1,4,3,2:T(8,128)(2,1)S(1)} %copy-done, bf16[32,4,18,1,7,2]{0,4,5,2,1,3:T(8,128)(2,1)S(1)} %slice.262, bf16[32,4,18,1,8,33]{0,4,5,2,1,3:T(8,128)(2,1)} %copy.321, ...), kind=kOutput, calls=%fused_computation.44 | convolution fusion | flops 941395968 | bytes 7880200 | tf_op jit(solution)/shard_map/conv_general_dilated | solution.py:26
  99.0 3.3 reduce_sum.36
  104.2 3.3 collective-permute-start.4
  107.5 1.9 collective-permute-start.5
  109.5 3.1 copy.334
  112.5 2.3 slice.268
  114.9 5.1 copy.419
  120.0 5.1 copy.349
  125.1 1.6 pad_maximum_fusion
  126.7 11.1 %select_maximum_fusion = bf16[32,4,18,258]{3,0,2,1:T(8,128)(2,1)} fusion(bf16[32,4,1,256]{3,0,2,1:T(8,128)(2,1)S(1)} %collective-permute-done.3, bf16[32,4,1,256]{3,0,2,1:T(8,128)(2,1)S(1)} %collective-permute-done.2, bf16[32,1,16,256]{3,0,2,1:T(8,128)(2,1)S(1)} %collective-permute-done.1, bf16[32,2,16,256]{3,0,2,1:T(8,128)(2,1)S(1)} %bitcast.630, ...), kind=kLoop, calls=%fused_computation.77 | loop fusion | flops 10699776 | bytes 2368512 | tf_op jit(solution)/shard_map/concatenate | solution.py:14
  139.5 2.4 copy.333
  141.9 2.4 multiply_convert_fusion
  154.4 1.7 fusion.66
  167.0 1.5 fusion.58
  180.7 1.8 pad_maximum_fusion.5
  182.9 36.2 %psum.31 = f32[16]{0:T(128)S(1)} all-reduce(f32[16]{0:T(128)S(1)} %convert_reduce_fusion.1), channel_id=1, replica_groups=mesh['sx'=8,'sy'=8,'rep'=2] {'sx','rep'}, use_global_device_ids=true, to_apply=%region_8.9 | all-reduce | flops 16 | bytes 128 | tf_op jit(solution)/shard_map/psum | solution.py:83
  219.7 66.4 %psum.29 = f32[64]{0:T(128)S(1)} all-reduce(f32[64]{0:T(128)S(1)} %get-tuple-element.30), channel_id=1, replica_groups=mesh['sx'=8,'sy'=8,'rep'=2] {'sx','sy','rep'}, use_global_device_ids=true, to_apply=%region_5.6 | all-reduce | flops 64 | bytes 512 | tf_op jit(solution)/shard_map/psum | solution.py:88
  286.6 41.3 %all-reduce.6.cloned.1.call-done = f32[64,32,3,3,3]{0,1,4,3,2:T(8,128)} async-done(((f32[64,32,3,3,3]{0,1,4,3,2:T(8,128)}), f32[64,32,3,3,3]{0,1,4,3,2:T(8,128)}) %all-reduce.6.cloned.1.call-update) | async-done | bytes 221200 | tf_op jit(solution)/shard_map/psum | solution.py:88
  327.9 1.8 broadcast_multiply_fusion
  329.7 40.3 %all-gather.2.cloned.1.call-done = bf16[64,3,64,128]{3,0,2,1:T(8,128)(2,1)} async-done(((bf16[64,3,8,128]{3,0,2,1:T(8,128)(2,1)}), bf16[64,3,64,128]{3,0,2,1:T(8,128)(2,1)}) %all-gather.2.cloned.1.call-update) | async-done | bytes 3145744 | tf_op jit(solution)/shard_map/all_gather | solution.py:72
  370.0 1.8 fusion.107
  385.5 5.5 %pad_bitcast_fusion = bf16[64,3,66,1,130]{4,0,2,1,3:T(8,128)(2,1)} fusion(bf16[64,3,64,128]{3,0,2,1:T(8,128)(2,1)S(1)} %copy-done.2), kind=kLoop, calls=%fused_computation.24 | loop fusion | bytes 6440448 | tf_op jit(solution)/shard_map/broadcast_in_dim | solution.py:27
  391.0 14.8 %copy.420 = bf16[64,3,66,1,130]{2,0,4,1,3:T(8,128)(2,1)} copy(bf16[64,3,66,1,130]{4,0,2,1,3:T(8,128)(2,1)} %pad_bitcast_fusion) | data formatting | bytes 6589440
  405.8 7.5 %pad.17.clone = bf16[64,3,66,1,136]{2,0,4,1,3:T(8,128)(2,1)} pad(bf16[64,3,66,1,130]{2,0,4,1,3:T(8,128)(2,1)} %copy.420, bf16[]{:T(256)} %constant.6.clone.1), padding=0_0x0_0x0_0x0_0x0_6 | pad | bytes 6741506 | tf_op jit(solution)/shard_map/broadcast_in_dim | solution.py:27
  413.3 11.8 %copy.326 = bf16[64,3,66,1,8,17]{0,4,5,2,1,3:T(8,128)(2,1)} copy(bf16[64,3,66,1,8,17]{2,0,5,4,1,3:T(8,128)(2,1)} %bitcast.623) | data formatting | bytes 6893568 | tf_op jit(solution)/shard_map/conv_general_dilated | solution.py:26
  425.1 1.4 slice.264
  426.5 19.6 %fusion.9 = f32[1,64,8,17,16]{4,2,3,1,0:T(8,128)} fusion(bf16[16,64,3,3,3]{1,0,4,3,2:T(8,128)(2,1)S(1)} %copy-done.18, bf16[64,3,66,1,7,2]{0,4,5,2,1,3:T(8,128)(2,1)S(1)} %slice.264, bf16[64,3,66,1,8,17]{0,4,5,2,1,3:T(8,128)(2,1)} %copy.326), kind=kOutput, calls=%fused_computation.36 | convolution fusion | flops 492853248 | bytes 4413952 | tf_op jit(solution)/shard_map/conv_general_dilated | solution.py:26
  446.1 3.2 copy.327
  450.9 75.9 %all-reduce.8.cloned.1.call-done = f32[16,64,3,3,3]{1,0,4,3,2:T(8,128)} async-done(((f32[16,64,3,3,3]{1,0,4,3,2:T(8,128)}), f32[16,64,3,3,3]{1,0,4,3,2:T(8,128)}) %all-reduce.8.cloned.1.call-update) | async-done | bytes 110608 | tf_op jit(solution)/shard_map/psum | solution.py:83
  526.7 1.6 broadcast_multiply_fusion.1
  (133 shorter events, 61.8 us)
Async XLA Ops:
  7.2 78.2 %copy-start = (bf16[64,32,3,3,3]{0,1,4,3,2:T(8,128)(2,1)S(1)}, bf16[64,32,3,3,3]{0,1,4,3,2:T(8,128)(2,1)}, u32[]{:S(2)}) copy-start(bf16[64,32,3,3,3]{0,1,4,3,2:T(8,128)(2,1)} %param.7) | copy-start | bytes 331780
  7.2 130.7 %reduce-scatter.2.cloned.1.call-start = ((), (), s32[]{:S(2)}) async-start(), calls=%async_computation.2 | async-start | bytes 4718592 | tf_op jit(solution)/shard_map/reduce_scatter | solution.py:82
  8.7 11.0 %collective-permute-start.6 = (bf16[16,1,64,128]{2,0,3,1:T(8,128)(2,1)S(1)}, bf16[16,1,64,128]{2,0,3,1:T(8,128)(2,1)S(1)}, u32[]{:S(2)}, u32[]{:S(2)}) collective-permute-start(bf16[16,1,64,128]{2,0,3,1:T(8,128)(2,1)S(1)} %bitcast.641), channel_id=1, source_target_pairs={{0,16},{16,32},{32,48},{48,64},{64,80},{80,96},{96,112},{1,17},{17... | collective-permute-start | bytes 786440 | tf_op jit(solution)/shard_map/ppermute | solution.py:16
  13.6 10.5 %collective-permute-start.7 = (bf16[16,1,64,128]{2,0,3,1:T(8,128)(2,1)S(1)}, bf16[16,1,64,128]{2,0,3,1:T(8,128)(2,1)S(1)}, u32[]{:S(2)}, u32[]{:S(2)}) collective-permute-start(bf16[16,1,64,128]{2,0,3,1:T(8,128)(2,1)S(1)} %bitcast.642), channel_id=1, source_target_pairs={{16,0},{32,16},{48,32},{64,48},{80,64},{96,80},{112,96},{17,1},{33... | collective-permute-start | bytes 786440 | tf_op jit(solution)/shard_map/ppermute | solution.py:18
  25.9 7.5 %copy-start.17 = (bf16[16,64,3,3,3]{1,0,4,3,2:T(8,128)(2,1)S(1)}, bf16[16,64,3,3,3]{1,0,4,3,2:T(8,128)(2,1)}, u32[]{:S(2)}) copy-start(bf16[16,64,3,3,3]{1,0,4,3,2:T(8,128)(2,1)} %param.9) | copy-start | bytes 165892
  25.9 7.5 %copy-start.20 = (pred[8,17]{0,1:T(8,128)(4,1)S(1)}, pred[8,17]{0,1:T(8,128)(4,1)}, u32[]{:S(2)}) copy-start(pred[8,17]{0,1:T(8,128)(4,1)} %constant.43) | copy-start | bytes 412
  46.3 1.0 copy-start.10
  46.3 281.6 %all-reduce.6.cloned.1.call-start = ((), (), s32[]{:S(2)}) async-start(), calls=%async_computation.3 | async-start | bytes 884736 | tf_op jit(solution)/shard_map/psum | solution.py:88
  47.7 5.2 collective-permute-start
  49.6 8.0 %collective-permute-start.1 = (bf16[32,1,16,256]{3,0,2,1:T(8,128)(2,1)S(1)}, bf16[32,1,16,256]{3,0,2,1:T(8,128)(2,1)S(1)}, u32[]{:S(2)}, u32[]{:S(2)}) collective-permute-start(bf16[32,1,16,256]{3,0,2,1:T(8,128)(2,1)S(1)} %get-tuple-element.39), channel_id=1, source_target_pairs={{16,0},{32,16},{48,32},{64,48},{80,64},{96,80},{112,96},{17,1},{33... | collective-permute-start | bytes 786440 | tf_op jit(solution)/shard_map/ppermute | solution.py:18
  52.9 14.9 %copy-start.4 = (bf16[32,1,16,256]{3,0,2,1:T(8,128)(2,1)}, bf16[32,1,16,256]{3,0,2,1:T(8,128)(2,1)S(1)}, u32[]{:S(2)}) copy-start(bf16[32,1,16,256]{3,0,2,1:T(8,128)(2,1)S(1)} %collective-permute-done) | copy-start | bytes 786436
  57.6 5.9 %collective-permute-start.2 = (bf16[32,4,1,256]{3,0,2,1:T(8,128)(2,1)S(1)}, bf16[32,4,1,256]{3,0,2,1:T(8,128)(2,1)S(1)}, u32[]{:S(2)}, u32[]{:S(2)}) collective-permute-start(bf16[32,4,1,256]{3,0,2,1:T(8,128)(2,1)S(1)} %get-tuple-element.36), channel_id=1, source_target_pairs={{0,2},{2,4},{4,6},{6,8},{8,10},{10,12},{12,14},{1,3},{3,5},{5,7},{... | collective-permute-start | bytes 196616 | tf_op jit(solution)/shard_map/ppermute | solution.py:16
  60.8 6.9 %collective-permute-start.3 = (bf16[32,4,1,256]{3,0,2,1:T(8,128)(2,1)S(1)}, bf16[32,4,1,256]{3,0,2,1:T(8,128)(2,1)S(1)}, u32[]{:S(2)}, u32[]{:S(2)}) collective-permute-start(bf16[32,4,1,256]{3,0,2,1:T(8,128)(2,1)S(1)} %get-tuple-element.37), channel_id=1, source_target_pairs={{2,0},{4,2},{6,4},{8,6},{10,8},{12,10},{14,12},{3,1},{5,3},{7,5},{... | collective-permute-start | bytes 196616 | tf_op jit(solution)/shard_map/ppermute | solution.py:18
  75.0 10.4 %copy-start.15 = (f32[64]{0:T(128)S(1)}, f32[64]{0:T(128)}, u32[]{:S(2)}) copy-start(f32[64]{0:T(128)} %param.8) | copy-start | bytes 772
  75.0 10.4 %copy-start.19 = (pred[8,33]{0,1:T(8,128)(4,1)S(1)}, pred[8,33]{0,1:T(8,128)(4,1)}, u32[]{:S(2)}) copy-start(pred[8,33]{0,1:T(8,128)(4,1)} %constant.41) | copy-start | bytes 796
  104.2 76.5 %collective-permute-start.4 = (bf16[64,1,8,128]{3,0,2,1:T(8,128)(2,1)}, bf16[64,1,8,128]{3,0,2,1:T(8,128)(2,1)}, u32[]{:S(2)}, u32[]{:S(2)}) collective-permute-start(bf16[64,1,8,128]{3,0,2,1:T(8,128)(2,1)} %fusion.182), channel_id=1, source_target_pairs={{0,16},{16,32},{32,48},{48,64},{64,80},{80,96},{96,112},{1,17},{17... | collective-permute-start | bytes 393224 | tf_op jit(solution)/shard_map/ppermute | solution.py:16
  107.5 73.2 %collective-permute-start.5 = (bf16[64,1,8,128]{3,0,2,1:T(8,128)(2,1)}, bf16[64,1,8,128]{3,0,2,1:T(8,128)(2,1)}, u32[]{:S(2)}, u32[]{:S(2)}) collective-permute-start(bf16[64,1,8,128]{3,0,2,1:T(8,128)(2,1)} %fusion.182), channel_id=1, source_target_pairs={{16,0},{32,16},{48,32},{64,48},{80,64},{96,80},{112,96},{17,1},{33... | collective-permute-start | bytes 393224 | tf_op jit(solution)/shard_map/ppermute | solution.py:18
  120.0 5.1 copy-start.5
  141.8 2.4 copy-start.7
  141.9 3.7 copy-start.9
  145.5 3.8 copy-start.6
  149.3 3.8 copy-start.8
  151.9 9.2 %slice-start = ((s8[4325376]{0:T(1024)(128)(4,1)}), s8[4194304]{0:T(1024)(128)(4,1)S(1)}, s32[]{:S(2)}) async-start(s8[4325376]{0:T(1024)(128)(4,1)} %bitcast.635), calls=%async_computation.5 | async-start | bytes 8388608
  156.1 5.1 slice-start.1
  161.2 1.1 copy-start.11
  177.3 192.7 %copy-start.3 = (bf16[1,16,1,64,128]{4,3,2,1,0:T(8,128)(2,1)S(1)}, bf16[1,16,1,64,128]{4,3,2,1,0:T(8,128)(2,1)}, u32[]{:S(2)}) copy-start(bf16[1,16,1,64,128]{4,3,2,1,0:T(8,128)(2,1)} %param.11) | copy-start | bytes 786436
  179.9 0.8 copy-start.12
  180.7 189.4 %all-gather.2.cloned.1.call-start = ((), (), s32[]{:S(2)}) async-start(), calls=%async_computation.1 | async-start | bytes 3538944 | tf_op jit(solution)/shard_map/all_gather | solution.py:72
  182.6 344.2 %all-reduce.8.cloned.1.call-start = ((), (), s32[]{:S(2)}) async-start(), calls=%async_computation.4 | async-start | bytes 442368 | tf_op jit(solution)/shard_map/psum | solution.py:83
  370.0 2.2 copy-start.2
  384.7 0.8 copy-start.13
  413.3 13.2 %copy-start.18 = (bf16[16,64,3,3,3]{1,0,4,3,2:T(8,128)(2,1)S(1)}, bf16[16,64,3,3,3]{1,0,4,3,2:T(8,128)(2,1)}, u32[]{:S(2)}) copy-start(bf16[16,64,3,3,3]{1,0,4,3,2:T(8,128)(2,1)} %param.9) | copy-start | bytes 165892
  446.1 3.2 copy-start.14
  446.1 3.2 copy-start.16
  446.1 82.3 %copy-start.1 = (bf16[64,32,3,3,3]{0,1,4,3,2:T(8,128)(2,1)S(1)}, bf16[64,32,3,3,3]{0,1,4,3,2:T(8,128)(2,1)}, u32[]{:S(2)}) copy-start(bf16[64,32,3,3,3]{0,1,4,3,2:T(8,128)(2,1)} %param.7) | copy-start | bytes 331780
Sparse Core Ops, SparseCore 0:
  46.4 54.4 reduce-scatter.1
  180.8 147.0 all-reduce.5
  330.1 39.8 all-gather.1
  385.7 141.0 all-reduce.7
where the time goes:
time: 545 us; the launch traced here: 535 us
  waiting for transfers between devices  177 us (32%)
  blocking collectives  103 us (19%)
  local copies, waits for them, and re-layouts  97.9 us (18%)
  matrix products  90 us (17%)
  other arithmetic  31.6 us (6%)
  starting transfers between devices  21.1 us (4%)
  between operations  14.8 us (3%)
    psum x1, waiting for transfers between devices, per_device(): summed_w2, summed_b2 = lax.psum((local_w2, local_b2), ('sx', 'rep'))  75.9 us
    psum x1, blocking collectives, per_device(): summed_w1, summed_b1 = lax.psum((local_w1, local_b1), ('sx', 'sy', 'rep'))  66.4 us
    dot_general x54, matrix products, weight_terms(): jnp.einsum('oxyz,cxyz->oc', cotan, piece, preferred_element_type=jnp.floa...  48.6 us
    conv_general_dilated x11, local copies, waits for them, and re-layouts, convolve(): lax.conv_general_dilated(padded[None], kernel, (1, 1, 1), ((0, 0), (0, 0)...  45.9 us
    conv_general_dilated x3, matrix products, convolve(): lax.conv_general_dilated(padded[None], kernel, (1, 1, 1), ((0, 0), (0, 0)...  41.4 us
    psum x1, waiting for transfers between devices, per_device(): summed_w1, summed_b1 = lax.psum((local_w1, local_b1), ('sx', 'sy', 'rep'))  41.3 us
    all_gather x1, waiting for transfers between devices, per_device(): gathered = lax.all_gather(pooled_x, 'sy', axis=2, tiled=True)  40.3 us
    psum x1, blocking collectives, per_device(): summed_w2, summed_b2 = lax.psum((local_w2, local_b2), ('sx', 'rep'))  36.2 us
  transfers between devices with their start and end apart: 12, of which 9 were waited for; matrix products, arithmetic and copies ran while one was open for 33% of the time, Pallas kernels for 0%

commit v1 on v0

--- a/solution.py
+++ b/solution.py
@@ -85,7 +85,7 @@
     grad_pre = (spread * 0.125 * jnp.where(pre > 0, 1.0, 0.3)).astype(jnp.bfloat16)
     local_w1 = weight_terms(grad_pre, input_pad)
     local_b1 = jnp.sum(grad_pre.astype(jnp.float32), axis=(1, 2, 3))
-    summed_w1, summed_b1 = lax.psum((local_w1, local_b1), ("sx", "sy", "rep"))
+    summed_w1, summed_b1 = lax.psum(lax.psum((local_w1, local_b1), ("sy", "rep")), "sx")
     return (
         second_out[None],
         scale * summed_w1,

time: 545 us -> 534 us (0.980)
  blocking collectives: 103 us -> 88.8 us
  waiting for transfers between devices: 177 us -> 190 us
  other arithmetic: 31.6 us -> 21.9 us
    psum x1 -> x2, waiting for transfers between devices: 41.3 us -> 79.9 us  [the longest x1 79.9 us: per_device(): lax.psum((local_w1, local_b1), ('sy', 'rep'))]
    all_gather x1, waiting for transfers between devices: 40.3 us -> 14.5 us  [per_device(): gathered = lax.all_gather(pooled_x, 'sy', axis=2, tiled=True)]
    psum x1 -> x2, blocking collectives: 66.4 us -> 52.7 us  [the longest x1 30.8 us: per_device(): lax.psum((local_w1, local_b1), ('sy', 'rep'))]
    concatenate x3, other arithmetic: 14.5 us -> 5.48 us  [padded_2(): jnp.concatenate([lax.ppermute(tail, axis, [(i, (i + 1) % count) for i in...]
    unnamed x51 -> x53, local copies, waits for them, and re-layouts: 25.9 us -> 25.9 us
  transfers between devices with their start and end apart: 12 -> 13, of which waited for: 9 -> 9; matrix products, arithmetic and copies ran while one was open for 33% -> 24% of each run, Pallas kernels for 0% -> 0%
where the time goes in v1:
time: 534 us; the launch traced here: 525 us
  waiting for transfers between devices  190 us (36%)
  local copies, waits for them, and re-layouts  98.4 us (18%)
  matrix products  90.1 us (17%)
  blocking collectives  88.8 us (17%)
  other arithmetic  21.9 us (4%)
  starting transfers between devices  21.1 us (4%)
  between operations  14.6 us (3%)
    psum x1, waiting for transfers between devices, per_device(): lax.psum((local_w1, local_b1), ('sy', 'rep'))  79.9 us
    psum x1, waiting for transfers between devices, per_device(): summed_w2, summed_b2 = lax.psum((local_w2, local_b2), ('sx', 'rep'))  75.9 us
    dot_general x54, matrix products, weight_terms(): jnp.einsum('oxyz,cxyz->oc', cotan, piece, preferred_element_type=jnp.floa...  48.6 us
    conv_general_dilated x11, local copies, waits for them, and re-layouts, convolve(): lax.conv_general_dilated(padded[None], kernel, (1, 1, 1), ((0, 0), (0, 0)...  45.6 us
    conv_general_dilated x3, matrix products, convolve(): lax.conv_general_dilated(padded[None], kernel, (1, 1, 1), ((0, 0), (0, 0)...  41.5 us
    psum x1, blocking collectives, per_device(): summed_w2, summed_b2 = lax.psum((local_w2, local_b2), ('sx', 'rep'))  36 us
    psum x1, blocking collectives, per_device(): lax.psum((local_w1, local_b1), ('sy', 'rep'))  30.8 us
    unnamed x53, local copies, waits for them, and re-layouts  25.9 us
  transfers between devices with their start and end apart: 13, of which 9 were waited for; matrix products, arithmetic and copies ran while one was open for 24% of the time, Pallas kernels for 0%

profile of v1, /device:TPU:1, one launch (start us, length us, event | category | flops | bytes accessed | tf_op | source)
XLA Modules:
  0.0 525.0 jit_solution(4005464799906169024)
XLA Ops:
  7.2 1.4 copy.329
  8.7 4.9 collective-permute-start.6
  13.6 1.9 collective-permute-start.7
  15.5 4.2 collective-permute-done.6
  19.7 4.4 collective-permute-done.7
  24.1 1.5 fusion.45
  25.9 6.0 %copy.331 = bf16[16,3,66,1,8,17]{0,4,5,2,1,3:T(8,128)(2,1)} copy(bf16[16,3,66,1,8,17]{2,0,5,4,1,3:T(8,128)(2,1)S(1)} %bitcast.640) | data formatting | bytes 1723392 | tf_op jit(solution)/shard_map/conv_general_dilated | solution.py:26
  33.3 9.5 %broadcast_select_fusion = f32[1,64,8,17,64]{4,2,3,1,0:T(8,128)S(1)} fusion(pred[8,17]{0,1:T(8,128)(4,1)S(1)} %copy-done.21, bf16[16,64,3,3,3]{1,0,4,3,2:T(8,128)(2,1)S(1)} %copy-done.18, bf16[16,3,66,1,7,2]{0,4,5,2,1,3:T(8,128)(2,1)S(1)} %slice.266, bf16[16,3,66,1,8,17]{0,4,5,2,1,3:T(8,128)(2,1)} %copy.331), kind=kOutput, calls=%fused_computation.70 | convolution fusion | flops 484742656 | bytes 3234056 | tf_op jit(solution)/shard_map/conv_general_dilated | solution.py:26
  43.7 2.6 slice_bitcast_fusion.1
  47.6 1.9 collective-permute-start
  49.6 2.4 collective-permute-start.1
  52.9 4.7 collective-permute-done.1
  57.6 3.2 collective-permute-start.2
  62.1 1.4 collective-permute-done.2
  63.5 4.2 collective-permute-done.3
  67.7 1.6 fusion.276
  69.6 5.4 %reshape.246 = bf16[32,4,18,1,8,33]{5,4,0,2,1,3:T(8,128)(2,1)} reshape(bf16[32,4,18,1,264]{4,0,2,1,3:T(8,128)(2,1)S(1)} %pad.15) | data formatting | bytes 2433024 | tf_op jit(solution)/shard_map/conv_general_dilated | solution.py:26
  74.9 9.3 %copy.321 = bf16[32,4,18,1,8,33]{0,4,5,2,1,3:T(8,128)(2,1)} copy(bf16[32,4,18,1,8,33]{5,4,0,2,1,3:T(8,128)(2,1)} %reshape.246) | data formatting | bytes 2433024 | tf_op jit(solution)/shard_map/conv_general_dilated | solution.py:26
  85.3 12.5 %compare_select_fusion = (f32[2,16,8,33,64]{4,2,3,1,0:T(8,128)}, f32[2,16,8,33,64]{4,2,3,1,0:T(8,128)S(1)}, f32[2,16,8,33,64]{4,2,3,1,0:T(8,128)}) fusion(f32[64]{0:T(128)S(1)} %copy-done.16, bf16[64,32,3,3,3]{0,1,4,3,2:T(8,128)(2,1)S(1)} %copy-done, bf16[32,4,18,1,7,2]{0,4,5,2,1,3:T(8,128)(2,1)S(1)} %slice.262, bf16[32,4,18,1,8,33]{0,4,5,2,1,3:T(8,128)(2,1)} %copy.321, ...), kind=kOutput, calls=%fused_computation.44 | convolution fusion | flops 941395968 | bytes 7880200 | tf_op jit(solution)/shard_map/conv_general_dilated | solution.py:26
  99.0 3.3 reduce_sum.36
  102.2 1.9 copy.323
  104.2 3.1 copy.334
  107.2 2.3 slice.268
  109.5 5.2 copy.419
  114.6 5.2 copy.349
  119.8 1.7 pad_maximum_fusion
  121.5 3.0 select_maximum_fusion
  126.2 2.3 copy.333
  128.5 2.4 multiply_convert_fusion
  141.0 1.5 fusion.66
  153.3 1.7 fusion.58
  167.4 3.3 collective-permute-start.4
  170.7 1.9 collective-permute-start.5
  172.6 79.9 %all-reduce.7.cloned.1.call-done = f32[64,32,3,3,3]{0,1,4,3,2:T(8,128)} async-done(((f32[64,32,3,3,3]{0,1,4,3,2:T(8,128)}), f32[64,32,3,3,3]{0,1,4,3,2:T(8,128)}) %all-reduce.7.cloned.1.call-update) | async-done | bytes 221200 | tf_op jit(solution)/shard_map/psum | solution.py:88
  253.8 36.0 %psum.47 = f32[16]{0:T(128)S(1)} all-reduce(f32[16]{0:T(128)S(1)} %convert_reduce_fusion.1), channel_id=1, replica_groups=mesh['sx'=8,'sy'=8,'rep'=2] {'sx','rep'}, use_global_device_ids=true, to_apply=%region_10.11 | all-reduce | flops 16 | bytes 128 | tf_op jit(solution)/shard_map/psum | solution.py:83
  290.3 30.8 %psum.44 = f32[64]{0:T(128)S(1)} all-reduce(f32[64]{0:T(128)S(1)} %get-tuple-element.30), channel_id=1, replica_groups=mesh['sx'=8,'sy'=8,'rep'=2] {'sy','rep'}, use_global_device_ids=true, to_apply=%region_6.7 | all-reduce | flops 64 | bytes 512 | tf_op jit(solution)/shard_map/psum | solution.py:88
  321.1 21.9 %psum.45 = f32[64]{0:T(128)S(1)} all-reduce(f32[64]{0:T(128)S(1)} %psum.44), channel_id=1, replica_groups=mesh['sx'=8,'sy'=8,'rep'=2] {'sx'}, use_global_device_ids=true, to_apply=%region_7.8 | all-reduce | flops 64 | bytes 512 | tf_op jit(solution)/shard_map/psum | solution.py:88
  343.6 1.8 broadcast_multiply_fusion
  345.4 14.5 %all-gather.2.cloned.1.call-done = bf16[64,3,64,128]{3,0,2,1:T(8,128)(2,1)} async-done(((bf16[64,3,8,128]{3,0,2,1:T(8,128)(2,1)}), bf16[64,3,64,128]{3,0,2,1:T(8,128)(2,1)}) %all-gather.2.cloned.1.call-update) | async-done | bytes 3145744 | tf_op jit(solution)/shard_map/all_gather | solution.py:72
  359.9 1.8 fusion.107
  375.4 5.5 %pad_bitcast_fusion = bf16[64,3,66,1,130]{4,0,2,1,3:T(8,128)(2,1)} fusion(bf16[64,3,64,128]{3,0,2,1:T(8,128)(2,1)S(1)} %copy-done.2), kind=kLoop, calls=%fused_computation.24 | loop fusion | bytes 6440448 | tf_op jit(solution)/shard_map/broadcast_in_dim | solution.py:27
  380.9 14.8 %copy.420 = bf16[64,3,66,1,130]{2,0,4,1,3:T(8,128)(2,1)} copy(bf16[64,3,66,1,130]{4,0,2,1,3:T(8,128)(2,1)} %pad_bitcast_fusion) | data formatting | bytes 6589440
  395.6 7.5 %pad.17.clone = bf16[64,3,66,1,136]{2,0,4,1,3:T(8,128)(2,1)} pad(bf16[64,3,66,1,130]{2,0,4,1,3:T(8,128)(2,1)} %copy.420, bf16[]{:T(256)} %constant.6.clone.1), padding=0_0x0_0x0_0x0_0x0_6 | pad | bytes 6741506 | tf_op jit(solution)/shard_map/broadcast_in_dim | solution.py:27
  403.2 11.7 %copy.326 = bf16[64,3,66,1,8,17]{0,4,5,2,1,3:T(8,128)(2,1)} copy(bf16[64,3,66,1,8,17]{2,0,5,4,1,3:T(8,128)(2,1)} %bitcast.623) | data formatting | bytes 6893568 | tf_op jit(solution)/shard_map/conv_general_dilated | solution.py:26
  416.3 19.6 %fusion.9 = f32[1,64,8,17,16]{4,2,3,1,0:T(8,128)} fusion(bf16[16,64,3,3,3]{1,0,4,3,2:T(8,128)(2,1)S(1)} %copy-done.19, bf16[64,3,66,1,7,2]{0,4,5,2,1,3:T(8,128)(2,1)S(1)} %slice.264, bf16[64,3,66,1,8,17]{0,4,5,2,1,3:T(8,128)(2,1)} %copy.326), kind=kOutput, calls=%fused_computation.36 | convolution fusion | flops 492853248 | bytes 4413952 | tf_op jit(solution)/shard_map/conv_general_dilated | solution.py:26
  435.8 3.2 copy.327
  440.7 75.9 %all-reduce.11.cloned.1.call-done = f32[16,64,3,3,3]{1,0,4,3,2:T(8,128)} async-done(((f32[16,64,3,3,3]{1,0,4,3,2:T(8,128)}), f32[16,64,3,3,3]{1,0,4,3,2:T(8,128)}) %all-reduce.11.cloned.1.call-update) | async-done | bytes 110608 | tf_op jit(solution)/shard_map/psum | solution.py:83
  516.6 1.6 broadcast_multiply_fusion.1
  (139 shorter events, 62.2 us)
Async XLA Ops:
  7.2 78.1 %copy-start = (bf16[64,32,3,3,3]{0,1,4,3,2:T(8,128)(2,1)S(1)}, bf16[64,32,3,3,3]{0,1,4,3,2:T(8,128)(2,1)}, u32[]{:S(2)}) copy-start(bf16[64,32,3,3,3]{0,1,4,3,2:T(8,128)(2,1)} %param.7) | copy-start | bytes 331780
  7.2 117.4 %reduce-scatter.2.cloned.1.call-start = ((), (), s32[]{:S(2)}) async-start(), calls=%async_computation.2 | async-start | bytes 4718592 | tf_op jit(solution)/shard_map/reduce_scatter | solution.py:82
  8.7 11.0 %collective-permute-start.6 = (bf16[16,1,64,128]{2,0,3,1:T(8,128)(2,1)S(1)}, bf16[16,1,64,128]{2,0,3,1:T(8,128)(2,1)S(1)}, u32[]{:S(2)}, u32[]{:S(2)}) collective-permute-start(bf16[16,1,64,128]{2,0,3,1:T(8,128)(2,1)S(1)} %bitcast.641), channel_id=1, source_target_pairs={{0,16},{16,32},{32,48},{48,64},{64,80},{80,96},{96,112},{1,17},{17... | collective-permute-start | bytes 786440 | tf_op jit(solution)/shard_map/ppermute | solution.py:16
  13.6 10.5 %collective-permute-start.7 = (bf16[16,1,64,128]{2,0,3,1:T(8,128)(2,1)S(1)}, bf16[16,1,64,128]{2,0,3,1:T(8,128)(2,1)S(1)}, u32[]{:S(2)}, u32[]{:S(2)}) collective-permute-start(bf16[16,1,64,128]{2,0,3,1:T(8,128)(2,1)S(1)} %bitcast.642), channel_id=1, source_target_pairs={{16,0},{32,16},{48,32},{64,48},{80,64},{96,80},{112,96},{17,1},{33... | collective-permute-start | bytes 786440 | tf_op jit(solution)/shard_map/ppermute | solution.py:18
  25.9 7.4 %copy-start.18 = (bf16[16,64,3,3,3]{1,0,4,3,2:T(8,128)(2,1)S(1)}, bf16[16,64,3,3,3]{1,0,4,3,2:T(8,128)(2,1)}, u32[]{:S(2)}) copy-start(bf16[16,64,3,3,3]{1,0,4,3,2:T(8,128)(2,1)} %param.9) | copy-start | bytes 165892
  25.9 7.4 %copy-start.21 = (pred[8,17]{0,1:T(8,128)(4,1)S(1)}, pred[8,17]{0,1:T(8,128)(4,1)}, u32[]{:S(2)}) copy-start(pred[8,17]{0,1:T(8,128)(4,1)} %constant.43) | copy-start | bytes 412
  46.2 1.0 copy-start.11
  46.3 206.3 %all-reduce.7.cloned.1.call-start = ((), (), s32[]{:S(2)}) async-start(), calls=%async_computation.3 | async-start | bytes 884736 | tf_op jit(solution)/shard_map/psum | solution.py:88
  47.6 5.2 collective-permute-start
  49.6 8.0 %collective-permute-start.1 = (bf16[32,1,16,256]{3,0,2,1:T(8,128)(2,1)S(1)}, bf16[32,1,16,256]{3,0,2,1:T(8,128)(2,1)S(1)}, u32[]{:S(2)}, u32[]{:S(2)}) collective-permute-start(bf16[32,1,16,256]{3,0,2,1:T(8,128)(2,1)S(1)} %get-tuple-element.39), channel_id=1, source_target_pairs={{16,0},{32,16},{48,32},{64,48},{80,64},{96,80},{112,96},{17,1},{33... | collective-permute-start | bytes 786440 | tf_op jit(solution)/shard_map/ppermute | solution.py:18
  52.8 14.9 %copy-start.4 = (bf16[32,1,16,256]{3,0,2,1:T(8,128)(2,1)}, bf16[32,1,16,256]{3,0,2,1:T(8,128)(2,1)S(1)}, u32[]{:S(2)}) copy-start(bf16[32,1,16,256]{3,0,2,1:T(8,128)(2,1)S(1)} %collective-permute-done) | copy-start | bytes 786436
  57.6 5.9 %collective-permute-start.2 = (bf16[32,4,1,256]{3,0,2,1:T(8,128)(2,1)S(1)}, bf16[32,4,1,256]{3,0,2,1:T(8,128)(2,1)S(1)}, u32[]{:S(2)}, u32[]{:S(2)}) collective-permute-start(bf16[32,4,1,256]{3,0,2,1:T(8,128)(2,1)S(1)} %get-tuple-element.36), channel_id=1, source_target_pairs={{0,2},{2,4},{4,6},{6,8},{8,10},{10,12},{12,14},{1,3},{3,5},{5,7},{... | collective-permute-start | bytes 196616 | tf_op jit(solution)/shard_map/ppermute | solution.py:16
  60.8 6.9 %collective-permute-start.3 = (bf16[32,4,1,256]{3,0,2,1:T(8,128)(2,1)S(1)}, bf16[32,4,1,256]{3,0,2,1:T(8,128)(2,1)S(1)}, u32[]{:S(2)}, u32[]{:S(2)}) collective-permute-start(bf16[32,4,1,256]{3,0,2,1:T(8,128)(2,1)S(1)} %get-tuple-element.37), channel_id=1, source_target_pairs={{2,0},{4,2},{6,4},{8,6},{10,8},{12,10},{14,12},{3,1},{5,3},{7,5},{... | collective-permute-start | bytes 196616 | tf_op jit(solution)/shard_map/ppermute | solution.py:18
  74.9 10.3 %copy-start.16 = (f32[64]{0:T(128)S(1)}, f32[64]{0:T(128)}, u32[]{:S(2)}) copy-start(f32[64]{0:T(128)} %param.8) | copy-start | bytes 772
  74.9 10.3 %copy-start.20 = (pred[8,33]{0,1:T(8,128)(4,1)S(1)}, pred[8,33]{0,1:T(8,128)(4,1)}, u32[]{:S(2)}) copy-start(pred[8,33]{0,1:T(8,128)(4,1)} %constant.41) | copy-start | bytes 796
  114.6 5.2 copy-start.5
  128.5 2.4 copy-start.7
  128.5 3.7 copy-start.9
  132.1 3.8 copy-start.6
  135.9 3.8 copy-start.8
  138.5 9.0 %slice-start = ((s8[4325376]{0:T(1024)(128)(4,1)}), s8[4194304]{0:T(1024)(128)(4,1)S(1)}, s32[]{:S(2)}) async-start(s8[4325376]{0:T(1024)(128)(4,1)} %bitcast.635), calls=%async_computation.6 | async-start | bytes 8388608
  142.5 5.1 slice-start.1
  147.6 1.1 copy-start.12
  162.7 4.6 copy-start.10
  165.2 194.7 %copy-start.3 = (bf16[1,16,1,64,128]{4,3,2,1,0:T(8,128)(2,1)S(1)}, bf16[1,16,1,64,128]{4,3,2,1,0:T(8,128)(2,1)}, u32[]{:S(2)}) copy-start(bf16[1,16,1,64,128]{4,3,2,1,0:T(8,128)(2,1)} %param.11) | copy-start | bytes 786436
  166.5 0.8 copy-start.13
  167.3 176.3 %all-reduce.9.cloned.1.call-start = ((), (), s32[]{:S(2)}) async-start(), calls=%async_computation.4 | async-start | bytes 884736 | tf_op jit(solution)/shard_map/psum | solution.py:88
  167.4 85.2 %collective-permute-start.4 = (bf16[64,1,8,128]{3,0,2,1:T(8,128)(2,1)S(1)}, bf16[64,1,8,128]{3,0,2,1:T(8,128)(2,1)S(1)}, u32[]{:S(2)}, u32[]{:S(2)}) collective-permute-start(bf16[64,1,8,128]{3,0,2,1:T(8,128)(2,1)S(1)} %fusion.182), channel_id=1, source_target_pairs={{0,16},{16,32},{32,48},{48,64},{64,80},{80,96},{96,112},{1,17},{17... | collective-permute-start | bytes 393224 | tf_op jit(solution)/shard_map/ppermute | solution.py:16
  170.7 81.9 %collective-permute-start.5 = (bf16[64,1,8,128]{3,0,2,1:T(8,128)(2,1)S(1)}, bf16[64,1,8,128]{3,0,2,1:T(8,128)(2,1)S(1)}, u32[]{:S(2)}, u32[]{:S(2)}) collective-permute-start(bf16[64,1,8,128]{3,0,2,1:T(8,128)(2,1)S(1)} %fusion.182), channel_id=1, source_target_pairs={{16,0},{32,16},{48,32},{64,48},{80,64},{96,80},{112,96},{17,1},{33... | collective-permute-start | bytes 393224 | tf_op jit(solution)/shard_map/ppermute | solution.py:18
  252.6 107.3 %all-gather.2.cloned.1.call-start = ((), (), s32[]{:S(2)}) async-start(), calls=%async_computation.1 | async-start | bytes 3538944 | tf_op jit(solution)/shard_map/all_gather | solution.py:72
  253.4 263.1 %all-reduce.11.cloned.1.call-start = ((), (), s32[]{:S(2)}) async-start(), calls=%async_computation.5 | async-start | bytes 442368 | tf_op jit(solution)/shard_map/psum | solution.py:83
  359.9 2.2 copy-start.2
  374.6 0.8 copy-start.14
  403.2 13.1 %copy-start.19 = (bf16[16,64,3,3,3]{1,0,4,3,2:T(8,128)(2,1)S(1)}, bf16[16,64,3,3,3]{1,0,4,3,2:T(8,128)(2,1)}, u32[]{:S(2)}) copy-start(bf16[16,64,3,3,3]{1,0,4,3,2:T(8,128)(2,1)} %param.9) | copy-start | bytes 165892
  435.8 3.2 copy-start.15
  435.8 3.2 copy-start.17
  435.8 82.4 %copy-start.1 = (bf16[64,32,3,3,3]{0,1,4,3,2:T(8,128)(2,1)S(1)}, bf16[64,32,3,3,3]{0,1,4,3,2:T(8,128)(2,1)}, u32[]{:S(2)}) copy-start(bf16[64,32,3,3,3]{0,1,4,3,2:T(8,128)(2,1)} %param.7) | copy-start | bytes 331780
Sparse Core Ops, SparseCore 0:
  46.4 54.4 reduce-scatter.1
  167.4 85.0 all-reduce.6
  254.9 60.2 all-reduce.8
  317.3 42.5 all-gather.1
  375.5 141.0 all-reduce.10
